TPU v7x, 256 devices: a whole 4x4x8 slice. The times are simulated.
256 devices in a mesh: member: 32 (over x, y, core), grid: 8 (over z).
Axes of the slice: x: 4, y: 4, z: 8, core: 2. Of those that a mesh axis runs over, the one named last changes fastest.
Arguments:
- prior_ensemble: bfloat16 [512, 48, 32768], P('member', None, 'grid'), may hold values from -6 to 6
- measured_location: int32 [8, 32, 128], P('grid', 'member'), may hold values from 0 to 6143
- measured_tally: int32 [8, 32], P('grid', 'member'), may hold values from 32 to 128, as said below
- measured_reading: float32 [8, 32, 128], P('grid', 'member'), may hold values from -6 to 6
- measured_noise_sigma: float32 [8, 32, 128], P('grid', 'member'), may hold values from 0.5 to 20, as said below
Outputs:
- analysis: bfloat16 [512, 48, 32768], P('member', None, 'grid')
Inputs may be any that keep to these rules, and one draw needn't show every extreme that they name: `measured_location`: cell of the observation within its block of 48 rows and 128 columns. `measured_tally`: some block in every draw uses all 128 slots. `measured_noise_sigma`: positive error deviations.
All inputs are finite; a program needn't handle non-finite values.
Results may differ from a plain program's by a relative error of at most 0.0058.
Values may be sent and summed in bfloat16 or wider, within the bound.
A program may use at most 128 MiB of HBM per device.

v0:
```python
import jax
import jax.numpy as jnp
from jax import lax
from jax.sharding import PartitionSpec as P

HIGHEST_PRECISION = lax.Precision.HIGHEST


def whiten(hx_values, values, errors, obs_total):
    hx_float = hx_values.astype(jnp.float32)
    hx_mean = jnp.mean(hx_float, axis=0)
    usable = (jnp.arange(hx_values.shape[1], dtype=jnp.int32) < obs_total).astype(jnp.float32)
    scale_obs = usable / errors
    whitened = (hx_float - hx_mean) * scale_obs
    innovation = (values - hx_mean) * scale_obs
    return (whitened, innovation)


def transform_matrix(gram_total, drive_vector):
    members = gram_total.shape[0]
    identity = jnp.eye(members, dtype=jnp.float32)
    system = (members - 1.0) * identity + gram_total
    factor_low = jnp.linalg.cholesky(system)
    inverse = jax.scipy.linalg.solve_triangular(factor_low, identity, lower=True)
    inner = jnp.dot(inverse, drive_vector, precision=HIGHEST_PRECISION)
    mean_weight = jnp.dot(inverse.T, inner, precision=HIGHEST_PRECISION)
    spread = jnp.sqrt(members - 1.0) * inverse.T
    return (mean_weight[:, None] + spread).astype(jnp.bfloat16)


def local_sums(whitened, innovation):
    gram_local = lax.dot_general(
        whitened, whitened, (((1,), (1,)), ((), ())), precision=HIGHEST_PRECISION
    )
    drive_local = jnp.dot(whitened, innovation, precision=HIGHEST_PRECISION)
    return (gram_local, drive_local)


def reduce_gram(whitened, innovation):
    gram_local, drive_local = local_sums(whitened, innovation)
    gram_total, drive_vector = lax.psum((gram_local, drive_local), ("member", "grid"))
    return transform_matrix(gram_total, drive_vector)


def apply_block(state_block, transform):
    members, row_count, columns = state_block.shape
    flattened = state_block.reshape(members, row_count * columns)
    state_mean = jnp.mean(flattened.astype(jnp.float32), axis=0)
    anomalies = (flattened.astype(jnp.float32) - state_mean).astype(jnp.bfloat16)
    increment = lax.dot_general(
        transform, anomalies, (((0,), (0,)), ((), ())), preferred_element_type=jnp.float32
    )
    return (state_mean + increment).astype(jnp.bfloat16).reshape(members, row_count, columns)


def local(
    prior_ensemble, measured_location, measured_tally, measured_reading, measured_noise_sigma
):
    values = measured_reading[0, 0]
    errors = measured_noise_sigma[0, 0]
    obs_total = measured_tally[0, 0]
    shard_profiles = lax.all_to_all(
        prior_ensemble, "member", split_axis=2, concat_axis=0, tiled=True
    )
    members, row_count, columns = shard_profiles.shape
    hx_values = jnp.take(
        shard_profiles.reshape(members, row_count * columns), measured_location[0, 0], axis=1
    )
    whitened, innovation = whiten(hx_values, values, errors, obs_total)
    transform = reduce_gram(whitened, innovation)
    updated = apply_block(shard_profiles, transform)
    return lax.all_to_all(updated, "member", split_axis=0, concat_axis=2, tiled=True)


def solution(mesh):
    in_specs = (
        P("member", None, "grid"),
        P("grid", "member", None),
        P("grid", "member"),
        P("grid", "member", None),
        P("grid", "member", None),
    )
    out_specs = P("member", None, "grid")
    return jax.shard_map(local, mesh=mesh, in_specs=in_specs, out_specs=out_specs, check_vma=False)
```

profile of v0, /device:TPU:1, one launch (start us, length us, event | category | flops | bytes accessed | tf_op | source)
XLA Modules:
  0.0 763.0 jit_solution(7519993507879228197)
XLA Ops:
  6.5 19.4 %copy.19 = bf16[16,48,4096]{1,0,2:T(8,128)(2,1)} copy(bf16[16,48,4096]{2,1,0:T(8,128)(2,1)} %param.5) | data formatting | bytes 12582912 | tf_op args[0]
  25.9 31.8 %reshape.139 = bf16[32,2,49152]{2,1,0:T(2,128)(2,1)} reshape(bf16[4096,16,48]{2,1,0:T(8,128)(2,1)} %bitcast.111) | data formatting | bytes 12582912
  57.7 8.8 %all-to-all-start = ((bf16[32,2,49152]{2,1,0:T(2,128)(2,1)}), bf16[32,2,49152]{2,1,0:T(2,128)(2,1)}, u32[]{:S(2)}, u32[]{:S(2)}) async-start(bf16[32,2,49152]{2,1,0:T(2,128)(2,1)} %reshape.139), calls=%async_computation | async-start | bytes 12582912 | tf_op jit(solution)/shard_map/all_to_all | solution.py:62
  67.8 1.1 fusion.12
  68.9 74.8 %all-to-all-done = bf16[32,2,49152]{2,1,0:T(2,128)(2,1)} async-done(((bf16[32,2,49152]{2,1,0:T(2,128)(2,1)}), bf16[32,2,49152]{2,1,0:T(2,128)(2,1)}, u32[]{:S(2)}, u32[]{:S(2)}) %all-to-all-start) | async-done | bytes 6291488 | tf_op jit(solution)/shard_map/all_to_all | solution.py:62
  143.7 27.6 %reshape.140 = bf16[4096,16,48]{2,1,0:T(8,128)(2,1)} reshape(bf16[32,2,49152]{2,1,0:T(2,128)(2,1)} %all-to-all-done) | data formatting | bytes 12582912
  171.3 18.8 %copy.20 = bf16[16,48,32,128]{3,1,0,2:T(8,128)(2,1)} copy(bf16[16,48,32,128]{1,0,3,2:T(8,128)(2,1)} %bitcast.110) | data formatting | bytes 12582912 | tf_op jit(solution)/shard_map/all_to_all | solution.py:62
  190.1 7.1 copy.44
  197.1 8.7 %copy.21 = bf16[512,6144]{0,1:T(8,128)(2,1)} copy(bf16[512,6144]{1,0:T(8,128)(2,1)} %bitcast.119) | data formatting | bytes 12582912 | tf_op jit(solution)/shard_map/reshape | solution.py:47
  205.8 4.5 gather_fusion
  210.5 2.2 fusion.20
  213.1 88.8 %psum.15 = f32[512]{0:T(512)S(1)} all-reduce(f32[512]{0:T(512)S(1)} %bitcast.121), channel_id=1, replica_groups=mesh['member'=32,'grid'=8] {'member','grid'}, use_global_device_ids=true, to_apply=%region_11.12 | all-reduce | flops 512 | bytes 4096 | tf_op jit(solution)/shard_map/psum | solution.py:41
  301.8 4.1 convert_reduce_fusion
  306.6 173.9 %all-reduce.3.cloned.1.call-done = f32[512,512]{0,1:T(8,128)} async-done(((f32[512,512]{0,1:T(8,128)}), f32[512,512]{0,1:T(8,128)}) %all-reduce.3.cloned.1.call-update) | async-done | bytes 1048592 | tf_op jit(solution)/shard_map/psum | solution.py:41
  480.5 1.3 select_add_fusion
  482.1 1.4 fusion.6
  483.6 11.7 %cholesky.107 = f32[128,128]{1,0:T(8,128)S(1)} custom-call(f32[128,128]{1,0:T(8,128)S(1)} %cholesky.269), custom_call_target="Cholesky" | custom-call | tf_op jit(solution)/shard_map/jit(cholesky)/cholesky | solution.py:23
  495.4 9.8 %custom-call.31 = f32[1,128,128]{1,2,0:T(8,128)S(1)} custom-call(f32[1,128,128]{2,1,0:T(8,128)S(1)} %get-tuple-element.36), custom_call_target="InvertDiagBlocksLowerTriangular" | custom-call | tf_op jit(solution)/shard_map/jit(cholesky)/cholesky | solution.py:23
  505.9 11.9 %cholesky.221 = f32[128,128]{1,0:T(8,128)S(1)} custom-call(f32[128,128]{1,0:T(8,128)S(1)} %cholesky.273), custom_call_target="Cholesky" | custom-call | tf_op jit(solution)/shard_map/jit(cholesky)/cholesky | solution.py:23
  518.1 9.8 %custom-call.32 = f32[1,128,128]{1,2,0:T(8,128)S(1)} custom-call(f32[1,128,128]{2,1,0:T(8,128)S(1)} %get-tuple-element.34), custom_call_target="InvertDiagBlocksLowerTriangular" | custom-call | tf_op jit(solution)/shard_map/jit(cholesky)/cholesky | solution.py:23
  528.5 1.6 convolution_subtract_fusion.4
  530.7 13.2 %cholesky.242 = f32[128,128]{1,0:T(8,128)} custom-call(f32[128,128]{1,0:T(8,128)} %cholesky.278), custom_call_target="Cholesky" | custom-call | tf_op jit(solution)/shard_map/jit(cholesky)/cholesky | solution.py:23
  543.9 1.5 select_reduce_fusion.1
  545.4 1.6 copy.28
  546.9 0.8 constant_dynamic-update-slice_fusion
  547.8 11.3 %custom-call.33 = f32[1,128,128]{1,2,0:T(8,128)} custom-call(f32[1,128,128]{2,1,0:T(8,128)} %get-tuple-element.32), custom_call_target="InvertDiagBlocksLowerTriangular" | custom-call | tf_op jit(solution)/shard_map/jit(cholesky)/cholesky | solution.py:23
  559.1 1.1 convolution_dynamic-update-slice_fusion.1
  560.2 1.3 convolution_subtract_fusion.5
  561.5 12.1 %cholesky.259 = f32[128,128]{1,0:T(8,128)S(1)} custom-call(f32[128,128]{1,0:T(8,128)S(1)} %convolution_subtract_fusion.5), custom_call_target="Cholesky" | custom-call | tf_op jit(solution)/shard_map/jit(cholesky)/cholesky | solution.py:23
  575.0 0.7 compare_reduce_fusion.3
  576.3 1.3 compare_reduce_fusion
  580.2 1.1 select_select_fusion
  581.3 0.7 triangular_solve.100
  582.0 14.5 %while.1 = (s32[]{:T(128)}, f32[512,512]{0,1:T(8,128)}, s32[4,2]{0,1:T(2,128)S(1)}, f32[4,128,128]{2,1,0:T(8,128)}, s32[]{:T(128)}) while((s32[]{:T(128)}, f32[512,512]{0,1:T(8,128)}, s32[4,2]{0,1:T(2,128)S(1)}, f32[4,128,128]{2,1,0:T(8,128)}, s32[]{:T(128)}) %tuple.25), condition=%wide.while_cond, body=%wide.while_body.sunk | while | flops 2 | bytes 393829 | solution.py:24
  582.7 2.2 dynamic-slice.7
  586.3 2.2 dynamic-slice.7
  590.0 2.2 dynamic-slice.7
  593.6 2.2 dynamic-slice.7
  596.5 40.1 %custom-call.34 = f32[4,128,128]{1,2,0:T(8,128)S(1)} custom-call(f32[4,128,128]{2,1,0:T(8,128)} %get-tuple-element.12), custom_call_target="InvertDiagBlocksLowerTriangular" | custom-call | tf_op jit(solution)/shard_map/jit(_solve_triangular)/triangular_solve | solution.py:24
  637.0 1.6 convolution_subtract_fusion.1
  639.0 2.2 convolution_subtract_fusion
  641.7 2.5 convolution_subtract_fusion.2
  644.6 1.0 convolution_bitcast_fusion
  646.3 6.7 fusion.1
  653.0 4.7 copy.38
  657.7 81.4 %all_to_all.33 = bf16[512,48,128]{2,1,0:T(8,128)(2,1)S(1)} all-to-all(bf16[512,48,128]{2,1,0:T(8,128)(2,1)S(1)} %bitcast.116), channel_id=1, replica_groups=mesh['member'=32,'grid'=8] {'member'}, dimensions={0} | all-to-all | bytes 12582912 | tf_op jit(solution)/shard_map/all_to_all | solution.py:72
  739.0 6.7 copy.45
  745.7 10.3 %all_to_all.30 = bf16[16,48,4096]{2,1,0:T(8,128)(2,1)} reshape(bf16[16,48,32,128]{3,2,1,0:T(8,128)(2,1)} %bitcast.118) | data formatting | bytes 12582912 | tf_op jit(solution)/shard_map/all_to_all | solution.py:72
  (68 shorter events, 14.1 us)
Async XLA Ops:
  57.6 10.1 %copy-start.3 = (s32[1,1,128]{2,1,0:T(1,128)S(1)}, s32[1,1,128]{2,1,0:T(1,128)}, u32[]{:S(2)}) copy-start(s32[1,1,128]{2,1,0:T(1,128)} %param.6) | copy-start | bytes 1540
  57.7 86.1 %all-to-all-start = ((bf16[32,2,49152]{2,1,0:T(2,128)(2,1)}), bf16[32,2,49152]{2,1,0:T(2,128)(2,1)}, u32[]{:S(2)}, u32[]{:S(2)}) async-start(bf16[32,2,49152]{2,1,0:T(2,128)(2,1)} %reshape.139), calls=%async_computation | async-start | bytes 12582912 | tf_op jit(solution)/shard_map/all_to_all | solution.py:62
  66.4 414.0 %all-reduce.3.cloned.1.call-start = ((), (), s32[]{:S(2)}) async-start(), calls=%async_computation.2 | async-start | bytes 2097152 | tf_op jit(solution)/shard_map/psum | solution.py:41
  197.1 13.3 %copy-start.2 = (f32[1,1,128]{2,1,0:T(1,128)S(1)}, f32[1,1,128]{2,1,0:T(1,128)}, u32[]{:S(2)}) copy-start(f32[1,1,128]{2,1,0:T(1,128)} %param.9) | copy-start | bytes 1540
  197.1 15.6 %copy-start.4 = (f32[1,1,128]{2,1,0:T(1,128)S(1)}, f32[1,1,128]{2,1,0:T(1,128)}, u32[]{:S(2)}) copy-start(f32[1,1,128]{2,1,0:T(1,128)} %param.8) | copy-start | bytes 1540
  483.6 44.5 %copy-start = (f32[512,512]{1,0:T(8,128)}, f32[512,512]{1,0:T(8,128)S(1)}, u32[]{:S(2)}) copy-start(f32[512,512]{1,0:T(8,128)S(1)} %fusion.6) | copy-start | bytes 3145732
  528.5 117.8 %slice-start = ((s8[6291456]{0:T(1024)(128)(4,1)}), s8[2097152]{0:T(1024)(128)(4,1)S(1)}, s32[]{:S(2)}) async-start(s8[6291456]{0:T(1024)(128)(4,1)} %bitcast.113), calls=%async_computation.3 | async-start | bytes 4194304
  580.2 66.1 %copy-start.1 = (f32[6144]{0:T(1024)S(1)}, f32[6144]{0:T(1024)}, u32[]{:S(2)}) copy-start(f32[6144]{0:T(1024)} %multiply_bitcast_fusion) | copy-start | bytes 73732
  638.6 7.7 %slice-start.1 = ((s8[6291456]{0:T(1024)(128)(4,1)}), s8[4194304]{0:T(1024)(128)(4,1)S(1)}, s32[]{:S(2)}) async-start(s8[6291456]{0:T(1024)(128)(4,1)} %bitcast.113), calls=%async_computation.4 | async-start | bytes 8388608
Sparse Core Ops, SparseCore 0:
  212.8 267.5 all-reduce.2
where the time goes:
time: 773 us; the launch traced here: 763 us
  waiting for transfers between devices  249 us (32%)
  blocking collectives  170 us (22%)
  local copies, waits for them, and re-layouts  158 us (20%)
  other arithmetic  136 us (18%)
  matrix products  23.9 us (3%)
  between operations  17.1 us (2%)
  starting transfers between devices  8.8 us (1%)
    psum x1, waiting for transfers between devices, reduce_gram(): lax.psum((gram_local, drive_local), ('member', 'grid'))  174 us
    unnamed x19, local copies, waits for them, and re-layouts  90.5 us
    psum x1, blocking collectives, reduce_gram(): lax.psum((gram_local, drive_local), ('member', 'grid'))  88.8 us
    another operation x15, other arithmetic, transform_matrix(): factor_low = jnp.linalg.cholesky(system)  85.3 us
    all_to_all x1, blocking collectives, local(): lax.all_to_all(updated, 'member', split_axis=0, concat_axis=2, tiled=True)  81.4 us
    all_to_all x1, waiting for transfers between devices, local(): lax.all_to_all(prior_ensemble, 'member', split_axis=2, concat_axis=0, til...  74.8 us
    another operation x3, other arithmetic, transform_matrix(): jax.scipy.linalg.solve_triangular(factor_low, identity, lower=True)  41.8 us
    all_to_all x1, local copies, waits for them, and re-layouts, local(): lax.all_to_all(prior_ensemble, 'member', split_axis=2, concat_axis=0, til...  18.8 us
  transfers between devices with their start and end apart: 2, of which 2 were waited for; matrix products, arithmetic and copies ran while one was open for 1% of the time, Pallas kernels for 0%

commit v1 on v0

--- a/solution.py
+++ b/solution.py
@@ -69,7 +69,12 @@
     whitened, innovation = whiten(hx_values, values, errors, obs_total)
     transform = reduce_gram(whitened, innovation)
     updated = apply_block(shard_profiles, transform)
-    return lax.all_to_all(updated, "member", split_axis=0, concat_axis=2, tiled=True)
+    return jnp.concatenate(
+        lax.all_to_all(
+            jnp.stack(jnp.split(updated, lax.axis_size("member"), axis=0)), "member", 0, 0
+        ),
+        axis=2,
+    )
 
 
 def solution(mesh):

time: 773 us -> 756 us (0.978)
  local copies, waits for them, and re-layouts: 158 us -> 143 us
    all_to_all x2 -> x0, local copies, waits for them, and re-layouts: 17 us -> none  [local(): lax.all_to_all(updated, 'member', split_axis=0, concat_axis=2, tiled=True)]
    unnamed x19 -> x83, local copies, waits for them, and re-layouts: 90.5 us -> 88 us
where the time goes in v1:
time: 756 us; the launch traced here: 746 us
  waiting for transfers between devices  249 us (33%)
  blocking collectives  170 us (22%)
  local copies, waits for them, and re-layouts  143 us (19%)
  other arithmetic  136 us (18%)
  matrix products  22.3 us (3%)
  between operations  17.7 us (2%)
  starting transfers between devices  8.8 us (1%)
    psum x1, waiting for transfers between devices, reduce_gram(): lax.psum((gram_local, drive_local), ('member', 'grid'))  174 us
    psum x1, blocking collectives, reduce_gram(): lax.psum((gram_local, drive_local), ('member', 'grid'))  88.8 us
    unnamed x83, local copies, waits for them, and re-layouts  88 us
    another operation x15, other arithmetic, transform_matrix(): factor_low = jnp.linalg.cholesky(system)  85.2 us
    all_to_all x1, blocking collectives, local(): lax.all_to_all(jnp.stack(jnp.split(updated, lax.axis_size('member'), axis...  81.4 us
    all_to_all x1, waiting for transfers between devices, local(): lax.all_to_all(prior_ensemble, 'member', split_axis=2, concat_axis=0, til...  74.8 us
    another operation x3, other arithmetic, transform_matrix(): jax.scipy.linalg.solve_triangular(factor_low, identity, lower=True)  41.8 us
    all_to_all x1, local copies, waits for them, and re-layouts, local(): lax.all_to_all(prior_ensemble, 'member', split_axis=2, concat_axis=0, til...  18.8 us
  transfers between devices with their start and end apart: 2, of which 2 were waited for; matrix products, arithmetic and copies ran while one was open for 1% of the time, Pallas kernels for 0%

profile of v1, /device:TPU:1, one launch (start us, length us, event | category | flops | bytes accessed | tf_op | source)
XLA Modules:
  0.0 746.1 jit_solution(13497720181277325075)
XLA Ops:
  6.5 19.4 %copy.19 = bf16[16,48,4096]{1,0,2:T(8,128)(2,1)} copy(bf16[16,48,4096]{2,1,0:T(8,128)(2,1)} %param.5) | data formatting | bytes 12582912 | tf_op args[0]
  25.9 31.8 %reshape.208 = bf16[32,2,49152]{2,1,0:T(2,128)(2,1)} reshape(bf16[4096,16,48]{2,1,0:T(8,128)(2,1)} %bitcast.300) | data formatting | bytes 12582912
  57.7 8.8 %all-to-all-start = ((bf16[32,2,49152]{2,1,0:T(2,128)(2,1)}), bf16[32,2,49152]{2,1,0:T(2,128)(2,1)}, u32[]{:S(2)}, u32[]{:S(2)}) async-start(bf16[32,2,49152]{2,1,0:T(2,128)(2,1)} %reshape.208), calls=%async_computation | async-start | bytes 12582912 | tf_op jit(solution)/shard_map/all_to_all | solution.py:62
  67.8 1.1 fusion.11
  68.9 74.8 %all-to-all-done = bf16[32,2,49152]{2,1,0:T(2,128)(2,1)} async-done(((bf16[32,2,49152]{2,1,0:T(2,128)(2,1)}), bf16[32,2,49152]{2,1,0:T(2,128)(2,1)}, u32[]{:S(2)}, u32[]{:S(2)}) %all-to-all-start) | async-done | bytes 6291488 | tf_op jit(solution)/shard_map/all_to_all | solution.py:62
  143.7 27.6 %reshape.209 = bf16[4096,16,48]{2,1,0:T(8,128)(2,1)} reshape(bf16[32,2,49152]{2,1,0:T(2,128)(2,1)} %all-to-all-done) | data formatting | bytes 12582912
  171.3 18.8 %copy.20 = bf16[16,48,32,128]{3,1,0,2:T(8,128)(2,1)} copy(bf16[16,48,32,128]{1,0,3,2:T(8,128)(2,1)} %bitcast.299) | data formatting | bytes 12582912 | tf_op jit(solution)/shard_map/all_to_all | solution.py:62
  190.1 7.1 copy.76
  197.1 8.7 %copy.21 = bf16[512,6144]{0,1:T(8,128)(2,1)} copy(bf16[512,6144]{1,0:T(8,128)(2,1)} %bitcast.305) | data formatting | bytes 12582912 | tf_op jit(solution)/shard_map/reshape | solution.py:47
  205.8 4.5 gather_fusion
  210.5 2.2 fusion.19
  213.1 88.8 %psum.15 = f32[512]{0:T(512)S(1)} all-reduce(f32[512]{0:T(512)S(1)} %bitcast.339), channel_id=1, replica_groups=mesh['member'=32,'grid'=8] {'member','grid'}, use_global_device_ids=true, to_apply=%region_11.12 | all-reduce | flops 512 | bytes 4096 | tf_op jit(solution)/shard_map/psum | solution.py:41
  301.8 4.1 convert_reduce_fusion
  306.6 173.9 %all-reduce.3.cloned.1.call-done = f32[512,512]{0,1:T(8,128)} async-done(((f32[512,512]{0,1:T(8,128)}), f32[512,512]{0,1:T(8,128)}) %all-reduce.3.cloned.1.call-update) | async-done | bytes 1048592 | tf_op jit(solution)/shard_map/psum | solution.py:41
  480.5 1.3 select_add_fusion
  482.1 1.4 fusion.5
  483.6 11.7 %cholesky.107 = f32[128,128]{1,0:T(8,128)S(1)} custom-call(f32[128,128]{1,0:T(8,128)S(1)} %cholesky.269), custom_call_target="Cholesky" | custom-call | tf_op jit(solution)/shard_map/jit(cholesky)/cholesky | solution.py:23
  495.4 9.8 %custom-call.31 = f32[1,128,128]{1,2,0:T(8,128)S(1)} custom-call(f32[1,128,128]{2,1,0:T(8,128)S(1)} %get-tuple-element.68), custom_call_target="InvertDiagBlocksLowerTriangular" | custom-call | tf_op jit(solution)/shard_map/jit(cholesky)/cholesky | solution.py:23
  506.1 11.9 %cholesky.221 = f32[128,128]{1,0:T(8,128)S(1)} custom-call(f32[128,128]{1,0:T(8,128)S(1)} %cholesky.273), custom_call_target="Cholesky" | custom-call | tf_op jit(solution)/shard_map/jit(cholesky)/cholesky | solution.py:23
  518.1 9.8 %custom-call.32 = f32[1,128,128]{1,2,0:T(8,128)S(1)} custom-call(f32[1,128,128]{2,1,0:T(8,128)S(1)} %get-tuple-element.66), custom_call_target="InvertDiagBlocksLowerTriangular" | custom-call | tf_op jit(solution)/shard_map/jit(cholesky)/cholesky | solution.py:23
  528.4 1.6 convolution_subtract_fusion.4
  530.7 13.2 %cholesky.242 = f32[128,128]{1,0:T(8,128)} custom-call(f32[128,128]{1,0:T(8,128)} %cholesky.278), custom_call_target="Cholesky" | custom-call | tf_op jit(solution)/shard_map/jit(cholesky)/cholesky | solution.py:23
  543.9 1.5 select_reduce_fusion.1
  545.4 1.6 copy.28
  546.9 0.8 constant_dynamic-update-slice_fusion
  547.8 11.3 %custom-call.33 = f32[1,128,128]{1,2,0:T(8,128)} custom-call(f32[1,128,128]{2,1,0:T(8,128)} %get-tuple-element.64), custom_call_target="InvertDiagBlocksLowerTriangular" | custom-call | tf_op jit(solution)/shard_map/jit(cholesky)/cholesky | solution.py:23
  559.0 1.1 convolution_dynamic-update-slice_fusion.1
  560.2 1.3 convolution_subtract_fusion.5
  561.5 12.1 %cholesky.259 = f32[128,128]{1,0:T(8,128)S(1)} custom-call(f32[128,128]{1,0:T(8,128)S(1)} %convolution_subtract_fusion.5), custom_call_target="Cholesky" | custom-call | tf_op jit(solution)/shard_map/jit(cholesky)/cholesky | solution.py:23
  574.2 0.7 compare_reduce_fusion.1
  575.0 0.7 compare_reduce_fusion.2
  575.6 0.7 compare_reduce_fusion.3
  576.3 1.3 compare_reduce_fusion
  580.2 1.1 select_select_fusion
  581.3 0.7 triangular_solve.100
  582.0 14.5 %while.1 = (s32[]{:T(128)}, f32[512,512]{0,1:T(8,128)}, s32[4,2]{0,1:T(2,128)S(1)}, f32[4,128,128]{2,1,0:T(8,128)}, s32[]{:T(128)}) while((s32[]{:T(128)}, f32[512,512]{0,1:T(8,128)}, s32[4,2]{0,1:T(2,128)S(1)}, f32[4,128,128]{2,1,0:T(8,128)}, s32[]{:T(128)}) %tuple.55), condition=%wide.while_cond, body=%wide.while_body.sunk | while | flops 2 | bytes 393829 | solution.py:24
  582.6 2.2 dynamic-slice.7
  586.3 2.2 dynamic-slice.7
  589.9 2.2 dynamic-slice.7
  593.6 2.2 dynamic-slice.7
  596.5 40.1 %custom-call.34 = f32[4,128,128]{1,2,0:T(8,128)S(1)} custom-call(f32[4,128,128]{2,1,0:T(8,128)} %get-tuple-element.12), custom_call_target="InvertDiagBlocksLowerTriangular" | custom-call | tf_op jit(solution)/shard_map/jit(_solve_triangular)/triangular_solve | solution.py:24
  636.9 1.6 convolution_subtract_fusion.1
  639.0 2.3 convolution_subtract_fusion
  641.7 2.5 convolution_subtract_fusion.2
  644.6 1.0 convolution_bitcast_fusion
  646.3 5.0 add_convert_fusion
  654.1 81.4 %all_to_all.20 = bf16[32,16,48,128]{3,2,1,0:T(8,128)(2,1)S(1)} all-to-all(bf16[32,16,48,128]{3,2,1,0:T(8,128)(2,1)S(1)} %bitcast_dynamic-update-slice_fusion.1), channel_id=1, replica_groups=mesh['member'=32,'grid'=8] {'member'}, dimensions={0} | all-to-all | bytes 12582912 | tf_op jit(solution)/shard_map/all_to_all | solution.py:73
  735.5 3.6 copy_bitcast_fusion.1
  (132 shorter events, 15.0 us)
Async XLA Ops:
  57.6 10.1 %copy-start.3 = (s32[1,1,128]{2,1,0:T(1,128)S(1)}, s32[1,1,128]{2,1,0:T(1,128)}, u32[]{:S(2)}) copy-start(s32[1,1,128]{2,1,0:T(1,128)} %param.6) | copy-start | bytes 1540
  57.7 86.1 %all-to-all-start = ((bf16[32,2,49152]{2,1,0:T(2,128)(2,1)}), bf16[32,2,49152]{2,1,0:T(2,128)(2,1)}, u32[]{:S(2)}, u32[]{:S(2)}) async-start(bf16[32,2,49152]{2,1,0:T(2,128)(2,1)} %reshape.208), calls=%async_computation | async-start | bytes 12582912 | tf_op jit(solution)/shard_map/all_to_all | solution.py:62
  66.4 414.0 %all-reduce.3.cloned.1.call-start = ((), (), s32[]{:S(2)}) async-start(), calls=%async_computation.2 | async-start | bytes 2097152 | tf_op jit(solution)/shard_map/psum | solution.py:41
  197.1 13.3 %copy-start.2 = (f32[1,1,128]{2,1,0:T(1,128)S(1)}, f32[1,1,128]{2,1,0:T(1,128)}, u32[]{:S(2)}) copy-start(f32[1,1,128]{2,1,0:T(1,128)} %param.9) | copy-start | bytes 1540
  197.1 15.6 %copy-start.4 = (f32[1,1,128]{2,1,0:T(1,128)S(1)}, f32[1,1,128]{2,1,0:T(1,128)}, u32[]{:S(2)}) copy-start(f32[1,1,128]{2,1,0:T(1,128)} %param.8) | copy-start | bytes 1540
  483.6 44.5 %copy-start = (f32[512,512]{1,0:T(8,128)}, f32[512,512]{1,0:T(8,128)S(1)}, u32[]{:S(2)}) copy-start(f32[512,512]{1,0:T(8,128)S(1)} %fusion.5) | copy-start | bytes 3145732
  528.4 117.9 %slice-start = ((s8[6291456]{0:T(1024)(128)(4,1)}), s8[2097152]{0:T(1024)(128)(4,1)S(1)}, s32[]{:S(2)}) async-start(s8[6291456]{0:T(1024)(128)(4,1)} %bitcast.302), calls=%async_computation.3 | async-start | bytes 4194304
  580.2 66.1 %copy-start.1 = (f32[6144]{0:T(1024)S(1)}, f32[6144]{0:T(1024)}, u32[]{:S(2)}) copy-start(f32[6144]{0:T(1024)} %multiply_bitcast_fusion) | copy-start | bytes 73732
  638.5 7.8 %slice-start.1 = ((s8[6291456]{0:T(1024)(128)(4,1)}), s8[4194304]{0:T(1024)(128)(4,1)S(1)}, s32[]{:S(2)}) async-start(s8[6291456]{0:T(1024)(128)(4,1)} %bitcast.302), calls=%async_computation.4 | async-start | bytes 8388608
Sparse Core Ops, SparseCore 0:
  212.8 267.5 all-reduce.2
